TPU v7x, 256 devices: a whole 4x4x8 slice. The times are simulated.
256 devices in a mesh: rep: 4 (over y), blk: 64 (over x, z, core).
Axes of the slice: x: 4, y: 4, z: 8, core: 2. Of those that a mesh axis runs over, the one named last changes fastest.
Arguments:
- feats: bfloat16 [1024, 128, 256], P('blk'), may hold values from -6 to 6
- requests: int32 [64, 64], P('blk'), may hold values from 0 to 15
- tile_dest: int32 [64, 512], P('blk'), may hold values from 0 to 15, as said below
- tile_slot: int32 [64, 512], P('blk'), may hold values from 0 to 63, as said below
- tile_vals: bfloat16 [64, 512, 128, 128], P('blk', None, 'rep'), may hold values from -0.09375 to 0.09375
- w_self: bfloat16 [256, 256], replicated, may hold values from -0.375 to 0.375
- w_neigh: bfloat16 [256, 256], replicated, may hold values from -0.375 to 0.375
- bias: float32 [256], replicated, may hold values from -3 to 3
- cotangent: bfloat16 [1024, 128, 256], P('blk', 'rep'), may hold values from -6 to 6
Outputs:
- hidden: bfloat16 [1024, 128, 256], P('blk', 'rep')
- grad_self: float32 [256, 256], replicated
- grad_neigh: float32 [256, 256], replicated
- grad_bias: float32 [256], replicated
- feat_grad: bfloat16 [1024, 128, 256], P('blk', 'rep')
Inputs may be any that keep to these rules, and one draw needn't show every extreme that they name: `tile_slot`: for each reader b, every owner index is named by exactly 8 of its tiles. `tile_dest`: no two tiles of one reader have both the same destination block and the same owner.
All inputs are finite; a program needn't handle non-finite values.
Results may differ from a plain program's by a relative error of at most 0.015.
Values may be sent and summed in bfloat16 or wider, within the bound.
A program may use at most 128 MiB of HBM per device.

v0:
```python
import math
import jax
import jax.numpy as jnp
from jax import lax
from jax.sharding import PartitionSpec as P


def collect_blocks(arrivals, send_list, blk_dev):
    onehot = (send_list[:, None] == jnp.arange(blk_dev, dtype=jnp.int32)[None, :]).astype(
        jnp.float32
    )
    return jnp.einsum("rb,rjd->bjd", onehot, arrivals, precision=lax.Precision.HIGHEST)


def on_device(feats, requests, tile_dest, tile_slot, tile_vals, w_self, w_neigh, bias, cotangent):
    owners = lax.axis_size("blk")
    replicas = lax.axis_size("rep")
    blk_dev, tile_rows, features = feats.shape
    quarter = tile_rows // replicas
    per_owner = blk_dev // 2
    rep_index = lax.axis_index("rep")
    send_list = requests[0]
    slot_owner = tile_slot[0]
    ordering = jnp.argsort(slot_owner, stable=True)
    sorted_dest = jnp.take(tile_dest[0], ordering, axis=0)
    grouped = jnp.take(tile_vals[0], ordering, axis=0).reshape(
        owners, per_owner, quarter, tile_rows
    )
    dest_onehot = sorted_dest[:, None] == jnp.arange(blk_dev, dtype=jnp.int32)[None, :]
    own_rows = lax.dynamic_slice_in_dim(feats, rep_index * quarter, quarter, 1)
    outgoing = jnp.take(feats, send_list, axis=0)
    sources = lax.all_to_all(outgoing, "blk", split_axis=0, concat_axis=0, tiled=True)
    products = jnp.einsum("okij,ojd->okid", grouped, sources, preferred_element_type=jnp.float32)
    products = products.reshape(owners * per_owner, quarter * features)
    summed = jnp.dot(dest_onehot.astype(jnp.float32).T, products, precision=lax.Precision.HIGHEST)
    aggregate = summed.reshape(blk_dev, quarter, features).astype(jnp.bfloat16)
    row_count = blk_dev * quarter
    feat_rows = own_rows.reshape(row_count, features)
    agg_rows = aggregate.reshape(row_count, features)
    preact = jnp.dot(feat_rows, w_self, preferred_element_type=jnp.float32)
    preact = preact + jnp.dot(agg_rows, w_neigh, preferred_element_type=jnp.float32) + bias
    hidden = jax.nn.silu(preact).astype(jnp.bfloat16).reshape(blk_dev, quarter, features)
    gating = jax.nn.sigmoid(preact)
    grad_rows = cotangent.reshape(row_count, features).astype(jnp.float32)
    grad_pre = (grad_rows * gating * (1.0 + preact * (1.0 - gating))).astype(jnp.bfloat16)
    grad_scale = 1.0 / math.sqrt(owners * blk_dev * tile_rows)
    self_local = (
        jnp.einsum("nd,ne->de", feat_rows, grad_pre, preferred_element_type=jnp.float32)
        * grad_scale
    )
    neigh_local = (
        jnp.einsum("nd,ne->de", agg_rows, grad_pre, preferred_element_type=jnp.float32) * grad_scale
    )
    bias_local = jnp.sum(grad_pre.astype(jnp.float32), axis=0) * grad_scale
    grad_self, grad_neigh, grad_bias = lax.psum(
        (self_local, neigh_local, bias_local), ("rep", "blk")
    )
    back_rows = jnp.einsum(
        "ne,de->nd", grad_pre, w_neigh, preferred_element_type=jnp.float32
    ).astype(jnp.bfloat16)
    back_flat = back_rows.reshape(blk_dev, quarter * features)
    picked = jnp.dot(
        dest_onehot.astype(jnp.bfloat16), back_flat, preferred_element_type=jnp.float32
    ).astype(jnp.bfloat16)
    picked = picked.reshape(owners, per_owner, quarter, features)
    contributions = jnp.einsum(
        "okij,okid->ojd", grouped, picked, preferred_element_type=jnp.float32
    )
    self_term = jnp.einsum("ne,de->nd", grad_pre, w_self, preferred_element_type=jnp.float32)
    arrivals = lax.all_to_all(
        contributions.astype(jnp.bfloat16), "blk", split_axis=0, concat_axis=0, tiled=True
    ).astype(contributions.dtype)
    collected = collect_blocks(arrivals, send_list, blk_dev)
    neighbour = lax.psum_scatter(
        collected.astype(jnp.bfloat16), "rep", scatter_dimension=1, tiled=True
    ).astype(jnp.float32)
    feat_grad = (self_term.reshape(blk_dev, quarter, features) + neighbour).astype(jnp.bfloat16)
    return (hidden, grad_self, grad_neigh, grad_bias, feat_grad)


def solution(mesh):
    in_specs = (
        P("blk", None, None),
        P("blk", None),
        P("blk", None),
        P("blk", None),
        P("blk", None, "rep", None),
        P(),
        P(),
        P(),
        P("blk", "rep", None),
    )
    out_specs = (P("blk", "rep", None), P(), P(), P(), P("blk", "rep", None))
    return jax.shard_map(
        on_device, mesh=mesh, in_specs=in_specs, out_specs=out_specs, check_vma=False
    )
```

profile of v0, /device:TPU:2, one launch (start us, length us, event | category | flops | bytes accessed | tf_op | source)
XLA Modules:
  0.0 564.7 jit_solution(1460504856205556514)
XLA Ops:
  9.4 2.8 gather_fusion.2
  12.2 4.6 broadcast_select_fusion
  16.8 12.3 %all-to-all-start = ((bf16[64,128,256]{2,1,0:T(8,128)(2,1)}), bf16[64,128,256]{2,1,0:T(8,128)(2,1)}, u32[]{:S(2)}, u32[]{:S(2)}) async-start(bf16[64,128,256]{2,1,0:T(8,128)(2,1)} %broadcast_select_fusion), calls=%async_computation | async-start | bytes 8388608 | tf_op jit(solution)/shard_map/all_to_all | solution.py:32
  29.3 3.8 sort.17
  33.0 3.5 gather_fusion
  36.7 5.5 gather_fusion.1
  42.4 81.6 %all-to-all-done = bf16[64,128,256]{2,1,0:T(8,128)(2,1)} async-done(((bf16[64,128,256]{2,1,0:T(8,128)(2,1)}), bf16[64,128,256]{2,1,0:T(8,128)(2,1)}, u32[]{:S(2)}, u32[]{:S(2)}) %all-to-all-start) | async-done | bytes 4194336 | tf_op jit(solution)/shard_map/all_to_all | solution.py:32
  124.0 4.9 convolution_bitcast_fusion
  128.9 17.9 %copy.29 = f32[64,8,32,256]{3,1,2,0:T(8,128)} copy(f32[64,8,32,256]{3,2,1,0:T(8,128)S(1)} %convolution_bitcast_fusion) | data formatting | bytes 33554432
  146.8 17.5 %copy.21 = f32[8192,512]{1,0:T(8,128)} copy(f32[8192,512]{0,1:T(8,128)} %bitcast.56) | data formatting | bytes 33554432 | tf_op jit(solution)/shard_map/dot_general | solution.py:35
  164.3 11.3 %convolution_convert_fusion.1 = bf16[16,32,256]{2,0,1:T(8,128)(2,1)S(1)} fusion(f32[32,256,512]{2,1,0:T(8,128)} %bitcast.55, s32[512]{0:T(512)S(1)} %get-tuple-element.26), kind=kOutput, calls=%fused_computation.18 | convolution fusion | flops 805445632 | bytes 17041408 | tf_op jit(solution)/shard_map/dot_general | solution.py:35
  175.7 1.1 convert_reduce_fusion
  177.3 5.6 convolution_convert_fusion
  182.9 8.3 %bitcast_convert_fusion = bf16[64,128,256]{2,1,0:T(8,128)(2,1)} fusion(bf16[64,8,32,256]{3,1,2,0:T(8,128)(2,1)} %bitcast.59, bf16[64,8,32,128]{3,2,1,0:T(8,128)(2,1)S(1)} %bitcast.58, pred[64,8]{1,0:T(8,128)(4,1)S(1)} %broadcast_in_dim.36), kind=kOutput, calls=%fused_computation.5 | convolution fusion | flops 1077936128 | bytes 16777728 | tf_op jit(solution)/shard_map/okij,okid->ojd/dot_general | solution.py:66
  191.2 101.4 %all_to_all.10 = bf16[64,128,256]{2,1,0:T(8,128)(2,1)S(1)} all-to-all(bf16[64,128,256]{2,1,0:T(8,128)(2,1)} %bitcast_convert_fusion), channel_id=1, replica_groups=mesh['rep'=4,'blk'=64] {'blk'}, dimensions={0} | all-to-all | bytes 8388608 | tf_op jit(solution)/shard_map/all_to_all | solution.py:70
  292.6 3.3 fusion.9
  296.0 1.0 convolution_multiply_fusion
  297.0 1.0 convolution_multiply_fusion.1
  298.2 76.7 %psum.23 = f32[256]{0:T(256)} all-reduce(f32[256]{0:T(256)S(1)} %broadcast_multiply_fusion), channel_id=1, replica_groups=mesh['rep'=4,'blk'=64] {'rep','blk'}, use_global_device_ids=true, to_apply=%region_4.5 | all-reduce | flops 256 | bytes 2048 | tf_op jit(solution)/shard_map/psum | solution.py:55
  374.9 1.2 fusion.15
  376.2 0.8 copy.26
  376.9 176.9 %all-reduce.3.cloned.1.call-done = (f32[256,256]{1,0:T(8,128)}, f32[256,256]{1,0:T(8,128)}) async-done(((f32[256,256]{1,0:T(8,128)}, f32[256,256]{1,0:T(8,128)}), (f32[256,256]{1,0:T(8,128)}, f32[256,256]{1,0:T(8,128)})) %all-reduce.3.cloned.1.call-update) | async-done | bytes 524304 | tf_op jit(solution)/shard_map/psum | solution.py:55
  553.9 1.7 copy.43
  555.6 1.7 copy.44
  (40 shorter events, 2.7 us)
Async XLA Ops:
  8.0 1.4 copy-start
  16.8 12.4 %copy-start.6 = (s32[1,512]{1,0:T(1,128)S(1)}, s32[1,512]{1,0:T(1,128)}, u32[]{:S(2)}) copy-start(s32[1,512]{1,0:T(1,128)} %param.12) | copy-start | bytes 6148
  16.8 16.2 %copy-start.2 = (s32[1,512]{1,0:T(1,128)S(1)}, s32[1,512]{1,0:T(1,128)}, u32[]{:S(2)}) copy-start(s32[1,512]{1,0:T(1,128)} %param.11) | copy-start | bytes 6148
  16.8 107.2 %all-to-all-start = ((bf16[64,128,256]{2,1,0:T(8,128)(2,1)}), bf16[64,128,256]{2,1,0:T(8,128)(2,1)}, u32[]{:S(2)}, u32[]{:S(2)}) async-start(bf16[64,128,256]{2,1,0:T(8,128)(2,1)} %broadcast_select_fusion), calls=%async_computation | async-start | bytes 8388608 | tf_op jit(solution)/shard_map/all_to_all | solution.py:32
  29.2 345.7 %reduce-scatter.2.cloned.1.call-start = ((), (), s32[]{:S(2)}) async-start(), calls=%async_computation.3 | async-start | bytes 1310720 | tf_op jit(solution)/shard_map/reduce_scatter | solution.py:74
  36.7 5.5 copy-start.4
  164.3 11.4 %copy-start.5 = (bf16[256,256]{1,0:T(8,128)(2,1)S(1)}, bf16[256,256]{1,0:T(8,128)(2,1)}, u32[]{:S(2)}) copy-start(bf16[256,256]{1,0:T(8,128)(2,1)} %param.15) | copy-start | bytes 393220
  164.3 11.4 %copy-start.8 = (bf16[16,32,256]{2,1,0:T(8,128)(2,1)S(1)}, bf16[16,32,256]{2,1,0:T(8,128)(2,1)}, u32[]{:S(2)}) copy-start(bf16[16,32,256]{2,1,0:T(8,128)(2,1)} %param.17) | copy-start | bytes 786436
  164.3 11.4 %copy-start.9 = (f32[256]{0:T(256)S(1)}, f32[256]{0:T(256)}, u32[]{:S(2)}) copy-start(f32[256]{0:T(256)} %param.16) | copy-start | bytes 3076
  177.3 5.6 copy-start.3
  191.2 101.4 %copy-start.7 = (s32[1,64]{1,0:T(1,128)S(1)}, s32[1,64]{1,0:T(1,128)}, u32[]{:S(2)}) copy-start(s32[1,64]{1,0:T(1,128)} %param.10) | copy-start | bytes 772
  292.6 264.6 %copy-start.1 = (bf16[16,128,256]{2,1,0:T(8,128)(2,1)S(1)}, bf16[16,128,256]{2,1,0:T(8,128)(2,1)}, u32[]{:S(2)}) copy-start(bf16[16,128,256]{2,1,0:T(8,128)(2,1)} %param.9) | copy-start | bytes 3145732
  295.9 257.9 %all-reduce.3.cloned.1.call-start = ((), (), s32[]{:S(2)}) async-start(), calls=%async_computation.4 | async-start | bytes 1048576 | tf_op jit(solution)/shard_map/psum | solution.py:55
Sparse Core Ops, SparseCore 0:
  296.1 24.7 reduce-scatter.1
Sparse Core Ops, SparseCore 1:
  302.6 251.2 all-reduce.2
where the time goes:
time: 565 us
  waiting for transfers between devices  259 us (46%)
  blocking collectives  178 us (32%)
  local copies, waits for them, and re-layouts  51.6 us (9%)
  matrix products  37.3 us (7%)
  between operations  15.7 us (3%)
  starting transfers between devices  12.4 us (2%)
  other arithmetic  11.1 us (2%)
    psum x1, waiting for transfers between devices, on_device(): lax.psum((self_local, neigh_local, bias_local), ('rep', 'blk'))  177 us
    all_to_all x1, blocking collectives, on_device(): lax.all_to_all(contributions.astype(jnp.bfloat16), 'blk', split_axis=0, c...  101 us
    all_to_all x1, waiting for transfers between devices, on_device(): lax.all_to_all(outgoing, 'blk', split_axis=0, concat_axis=0, tiled=True)  81.6 us
    psum x1, blocking collectives, on_device(): lax.psum((self_local, neigh_local, bias_local), ('rep', 'blk'))  76.7 us
    unnamed x24, local copies, waits for them, and re-layouts  22.1 us
    dot_general x1, local copies, waits for them, and re-layouts, on_device(): jnp.dot(dest_onehot.astype(jnp.float32).T, products, precision=lax.Precis...  17.5 us
    all_to_all x1, starting transfers between devices, on_device(): lax.all_to_all(outgoing, 'blk', split_axis=0, concat_axis=0, tiled=True)  12.3 us
    dot_general x1, matrix products, on_device(): jnp.dot(dest_onehot.astype(jnp.float32).T, products, precision=lax.Precis...  11.3 us
  transfers between devices with their start and end apart: 3, of which 2 were waited for; matrix products, arithmetic and copies ran while one was open for 3% of the time, Pallas kernels for 0%

commit v1 on v0

--- a/solution.py
+++ b/solution.py
@@ -53,7 +53,7 @@
     )
     bias_local = jnp.sum(grad_pre.astype(jnp.float32), axis=0) * grad_scale
     grad_self, grad_neigh, grad_bias = lax.psum(
-        (self_local, neigh_local, bias_local), ("rep", "blk")
+        lax.psum((self_local, neigh_local, bias_local), "rep"), "blk"
     )
     back_rows = jnp.einsum(
         "ne,de->nd", grad_pre, w_neigh, preferred_element_type=jnp.float32

time: 565 us -> 518 us (0.917)
  blocking collectives: 178 us -> 116 us
  starting transfers between devices: 12.4 us -> 19.5 us
  waiting for transfers between devices: 259 us -> 265 us
    all_to_all x1 -> x0, blocking collectives: 101 us -> none  [on_device(): lax.all_to_all(contributions.astype(jnp.bfloat16), 'blk', split_axis=0, c...]
    all_to_all x0 -> x1, waiting for transfers between devices: none -> 92.8 us  [on_device(): lax.all_to_all(contributions.astype(jnp.bfloat16), 'blk', split_axis=0, c...]
    psum x1 -> x2, waiting for transfers between devices: 177 us -> 90.4 us  [the longest x1 90.4 us: on_device(): lax.psum(lax.psum((self_local, neigh_local, bias_local), 'rep'), 'blk')]
    psum x1 -> x2, blocking collectives: 76.7 us -> 116 us  [the longest x1 105 us: on_device(): lax.psum(lax.psum((self_local, neigh_local, bias_local), 'rep'), 'blk')]
    all_to_all x0 -> x1, starting transfers between devices: none -> 7.08 us  [on_device(): lax.all_to_all(contributions.astype(jnp.bfloat16), 'blk', split_axis=0, c...]
  transfers between devices with their start and end apart: 3 -> 5, of which waited for: 2 -> 3; matrix products, arithmetic and copies ran while one was open for 3% -> 4% of each run, Pallas kernels for 0% -> 0%
where the time goes in v1:
time: 518 us; the launch traced here: 517 us
  waiting for transfers between devices  265 us (51%)
  blocking collectives  116 us (22%)
  local copies, waits for them, and re-layouts  51.6 us (10%)
  matrix products  39.5 us (8%)
  starting transfers between devices  19.5 us (4%)
  between operations  14 us (3%)
  other arithmetic  11 us (2%)
    psum x1, blocking collectives, on_device(): lax.psum(lax.psum((self_local, neigh_local, bias_local), 'rep'), 'blk')  105 us
    all_to_all x1, waiting for transfers between devices, on_device(): lax.all_to_all(contributions.astype(jnp.bfloat16), 'blk', split_axis=0, c...  92.8 us
    psum x1, waiting for transfers between devices, on_device(): lax.psum(lax.psum((self_local, neigh_local, bias_local), 'rep'), 'blk')  90.4 us
    all_to_all x1, waiting for transfers between devices, on_device(): lax.all_to_all(outgoing, 'blk', split_axis=0, concat_axis=0, tiled=True)  81.7 us
    unnamed x24, local copies, waits for them, and re-layouts  22.1 us
    dot_general x1, local copies, waits for them, and re-layouts, on_device(): jnp.dot(dest_onehot.astype(jnp.float32).T, products, precision=lax.Precis...  17.5 us
    all_to_all x1, starting transfers between devices, on_device(): lax.all_to_all(outgoing, 'blk', split_axis=0, concat_axis=0, tiled=True)  12.3 us
    dot_general x1, matrix products, on_device(): jnp.dot(dest_onehot.astype(jnp.float32).T, products, precision=lax.Precis...  11.3 us
  transfers between devices with their start and end apart: 5, of which 3 were waited for; matrix products, arithmetic and copies ran while one was open for 4% of the time, Pallas kernels for 0%

profile of v1, /device:TPU:2, one launch (start us, length us, event | category | flops | bytes accessed | tf_op | source)
XLA Modules:
  0.0 517.1 jit_solution(12777980673085022481)
XLA Ops:
  8.6 2.8 gather_fusion.2
  11.4 4.6 broadcast_select_fusion
  16.0 12.3 %all-to-all-start = ((bf16[64,128,256]{2,1,0:T(8,128)(2,1)}), bf16[64,128,256]{2,1,0:T(8,128)(2,1)}, u32[]{:S(2)}, u32[]{:S(2)}) async-start(bf16[64,128,256]{2,1,0:T(8,128)(2,1)} %broadcast_select_fusion), calls=%async_computation | async-start | bytes 8388608 | tf_op jit(solution)/shard_map/all_to_all | solution.py:32
  28.4 3.8 sort.17
  32.2 3.5 gather_fusion
  35.8 5.5 %gather_fusion.1 = bf16[512,32,128]{2,1,0:T(8,128)(2,1)} fusion(bf16[512,32,128]{2,1,0:T(8,128)(2,1)} %bitcast.60, s32[1024]{0:T(1024)S(1)} %pad_clamp_fusion.1), kind=kCustom, calls=%fused_computation.1 | custom fusion | bytes 8390656 | tf_op jit(solution)/shard_map/jit(_take)/gather | solution.py:26
  41.5 81.7 %all-to-all-done = bf16[64,128,256]{2,1,0:T(8,128)(2,1)} async-done(((bf16[64,128,256]{2,1,0:T(8,128)(2,1)}), bf16[64,128,256]{2,1,0:T(8,128)(2,1)}, u32[]{:S(2)}, u32[]{:S(2)}) %all-to-all-start) | async-done | bytes 4194336 | tf_op jit(solution)/shard_map/all_to_all | solution.py:32
  123.2 4.9 convolution_bitcast_fusion
  128.1 17.9 %copy.29 = f32[64,8,32,256]{3,1,2,0:T(8,128)} copy(f32[64,8,32,256]{3,2,1,0:T(8,128)S(1)} %convolution_bitcast_fusion) | data formatting | bytes 33554432
  146.0 17.5 %copy.21 = f32[8192,512]{1,0:T(8,128)} copy(f32[8192,512]{0,1:T(8,128)} %bitcast.56) | data formatting | bytes 33554432 | tf_op jit(solution)/shard_map/dot_general | solution.py:35
  163.4 11.3 %convolution_convert_fusion.1 = bf16[16,32,256]{2,0,1:T(8,128)(2,1)S(1)} fusion(f32[32,256,512]{2,1,0:T(8,128)} %bitcast.55, s32[512]{0:T(512)S(1)} %get-tuple-element.28), kind=kOutput, calls=%fused_computation.18 | convolution fusion | flops 805445632 | bytes 17041408 | tf_op jit(solution)/shard_map/dot_general | solution.py:35
  174.9 1.1 convert_reduce_fusion
  176.4 5.6 %convolution_convert_fusion = bf16[512,8192]{1,0:T(8,128)(2,1)} fusion(bf16[16,8192]{1,0:T(8,128)(2,1)S(1)} %reshape.89, s32[512]{0:T(512)S(1)} %get-tuple-element.28), kind=kOutput, calls=%fused_computation.3 | convolution fusion | flops 138420224 | bytes 8652800 | tf_op jit(solution)/shard_map/dot_general | solution.py:62
  182.0 8.3 %bitcast_convert_fusion = bf16[64,128,256]{2,1,0:T(8,128)(2,1)} fusion(bf16[64,8,32,256]{3,1,2,0:T(8,128)(2,1)} %bitcast.59, bf16[64,8,32,128]{3,2,1,0:T(8,128)(2,1)S(1)} %bitcast.58, pred[64,8]{1,0:T(8,128)(4,1)S(1)} %broadcast_in_dim.36), kind=kOutput, calls=%fused_computation.5 | convolution fusion | flops 1077936128 | bytes 16777728 | tf_op jit(solution)/shard_map/okij,okid->ojd/dot_general | solution.py:66
  190.4 7.1 %all-to-all-start.1 = ((bf16[64,128,256]{2,1,0:T(8,128)(2,1)}), bf16[64,128,256]{2,1,0:T(8,128)(2,1)}, u32[]{:S(2)}, u32[]{:S(2)}) async-start(bf16[64,128,256]{2,1,0:T(8,128)(2,1)} %bitcast_convert_fusion), calls=%async_computation.1 | async-start | bytes 8388608 | tf_op jit(solution)/shard_map/all_to_all | solution.py:70
  197.5 1.0 convolution_multiply_fusion
  199.5 92.8 %all-to-all-done.1 = bf16[64,128,256]{2,1,0:T(8,128)(2,1)} async-done(((bf16[64,128,256]{2,1,0:T(8,128)(2,1)}), bf16[64,128,256]{2,1,0:T(8,128)(2,1)}, u32[]{:S(2)}, u32[]{:S(2)}) %all-to-all-start.1) | async-done | bytes 4194336 | tf_op jit(solution)/shard_map/all_to_all | solution.py:70
  292.3 5.6 %fusion.9 = bf16[16,128,256]{2,0,1:T(8,128)(2,1)} fusion(bf16[64,128,256]{2,1,0:T(8,128)(2,1)} %all-to-all-done.1, s32[64]{0:T(128)S(1)} %bitcast.67), kind=kOutput, calls=%fused_computation.15 | convolution fusion | flops 67634176 | bytes 5243136 | tf_op jit(solution)/shard_map/rb,rjd->bjd/dot_general | solution.py:12
  298.7 10.8 %psum.46 = f32[256]{0:T(256)S(1)} all-reduce(f32[256]{0:T(256)S(1)} %broadcast_multiply_fusion), channel_id=1, replica_groups=mesh['rep'=4,'blk'=64] {'rep'}, use_global_device_ids=true, to_apply=%region_6.7 | all-reduce | flops 256 | bytes 2048 | tf_op jit(solution)/shard_map/psum | solution.py:56
  309.5 105.3 %psum.47 = f32[256]{0:T(256)} all-reduce(f32[256]{0:T(256)S(1)} %psum.46), channel_id=1, replica_groups=mesh['rep'=4,'blk'=64] {'blk'}, use_global_device_ids=true, to_apply=%region_7.8 | all-reduce | flops 256 | bytes 2048 | tf_op jit(solution)/shard_map/psum | solution.py:55
  414.8 1.2 fusion.15
  416.8 90.4 %all-reduce.5.cloned.1.call-done = (f32[256,256]{1,0:T(8,128)}, f32[256,256]{1,0:T(8,128)}) async-done(((f32[256,256]{1,0:T(8,128)}, f32[256,256]{1,0:T(8,128)}), (f32[256,256]{1,0:T(8,128)}, f32[256,256]{1,0:T(8,128)})) %all-reduce.5.cloned.1.call-update) | async-done | bytes 524304 | tf_op jit(solution)/shard_map/psum | solution.py:55
  507.2 1.7 copy.45
  508.9 1.7 copy.46
  (45 shorter events, 4.9 us)
Async XLA Ops:
  7.2 1.4 copy-start
  16.0 12.4 %copy-start.6 = (s32[1,512]{1,0:T(1,128)S(1)}, s32[1,512]{1,0:T(1,128)}, u32[]{:S(2)}) copy-start(s32[1,512]{1,0:T(1,128)} %param.12) | copy-start | bytes 6148
  16.0 16.2 %copy-start.2 = (s32[1,512]{1,0:T(1,128)S(1)}, s32[1,512]{1,0:T(1,128)}, u32[]{:S(2)}) copy-start(s32[1,512]{1,0:T(1,128)} %param.11) | copy-start | bytes 6148
  16.0 107.2 %all-to-all-start = ((bf16[64,128,256]{2,1,0:T(8,128)(2,1)}), bf16[64,128,256]{2,1,0:T(8,128)(2,1)}, u32[]{:S(2)}, u32[]{:S(2)}) async-start(bf16[64,128,256]{2,1,0:T(8,128)(2,1)} %broadcast_select_fusion), calls=%async_computation | async-start | bytes 8388608 | tf_op jit(solution)/shard_map/all_to_all | solution.py:32
  35.8 5.5 %copy-start.4 = (bf16[256,256]{1,0:T(8,128)(2,1)S(1)}, bf16[256,256]{1,0:T(8,128)(2,1)}, u32[]{:S(2)}) copy-start(bf16[256,256]{1,0:T(8,128)(2,1)} %param.14) | copy-start | bytes 393220
  163.4 11.4 %copy-start.5 = (bf16[256,256]{1,0:T(8,128)(2,1)S(1)}, bf16[256,256]{1,0:T(8,128)(2,1)}, u32[]{:S(2)}) copy-start(bf16[256,256]{1,0:T(8,128)(2,1)} %param.15) | copy-start | bytes 393220
  163.4 11.4 %copy-start.8 = (bf16[16,32,256]{2,1,0:T(8,128)(2,1)S(1)}, bf16[16,32,256]{2,1,0:T(8,128)(2,1)}, u32[]{:S(2)}) copy-start(bf16[16,32,256]{2,1,0:T(8,128)(2,1)} %param.17) | copy-start | bytes 786436
  163.4 11.4 %copy-start.9 = (f32[256]{0:T(256)S(1)}, f32[256]{0:T(256)}, u32[]{:S(2)}) copy-start(f32[256]{0:T(256)} %param.16) | copy-start | bytes 3076
  176.4 5.6 %copy-start.3 = (bf16[512,32,128]{2,1,0:T(8,128)(2,1)S(1)}, bf16[512,32,128]{2,1,0:T(8,128)(2,1)}, u32[]{:S(2)}) copy-start(bf16[512,32,128]{2,1,0:T(8,128)(2,1)} %gather_fusion.1) | copy-start | bytes 12582916
  190.4 102.0 %copy-start.7 = (s32[1,64]{1,0:T(1,128)S(1)}, s32[1,64]{1,0:T(1,128)}, u32[]{:S(2)}) copy-start(s32[1,64]{1,0:T(1,128)} %param.10) | copy-start | bytes 772
  190.4 101.9 %all-to-all-start.1 = ((bf16[64,128,256]{2,1,0:T(8,128)(2,1)}), bf16[64,128,256]{2,1,0:T(8,128)(2,1)}, u32[]{:S(2)}, u32[]{:S(2)}) async-start(bf16[64,128,256]{2,1,0:T(8,128)(2,1)} %bitcast_convert_fusion), calls=%async_computation.1 | async-start | bytes 8388608 | tf_op jit(solution)/shard_map/all_to_all | solution.py:70
  197.5 100.8 %all-reduce.7.cloned.1.call-start = ((), (), s32[]{:S(2)}) async-start(), calls=%async_computation.5 | async-start | bytes 1048576 | tf_op jit(solution)/shard_map/psum | solution.py:56
  199.5 215.3 %reduce-scatter.2.cloned.1.call-start = ((), (), s32[]{:S(2)}) async-start(), calls=%async_computation.3 | async-start | bytes 1310720 | tf_op jit(solution)/shard_map/reduce_scatter | solution.py:74
  292.3 218.3 %copy-start.1 = (bf16[16,128,256]{2,1,0:T(8,128)(2,1)S(1)}, bf16[16,128,256]{2,1,0:T(8,128)(2,1)}, u32[]{:S(2)}) copy-start(bf16[16,128,256]{2,1,0:T(8,128)(2,1)} %param.9) | copy-start | bytes 3145732
  298.0 209.3 %all-reduce.5.cloned.1.call-start = ((), (), s32[]{:S(2)}) async-start(), calls=%async_computation.4 | async-start | bytes 1048576 | tf_op jit(solution)/shard_map/psum | solution.py:55
Sparse Core Ops, SparseCore 0:
  201.3 49.4 all-reduce.6
  298.1 23.8 reduce-scatter.1
  326.0 181.2 all-reduce.4
